TPU v7x, 32 devices: a whole 2x2x4 slice. The times are simulated.
32 devices in a mesh: dp: 8 (over z, y), tensor: 4 (over x, core).
Axes of the slice: x: 2, y: 2, z: 4, core: 2. Of those that a mesh axis runs over, the one named last changes fastest.
Arguments:
- tokens: bfloat16 [12288, 768], P('dp'), may hold values from -6 to 6
- segment_ids: int32 [24, 512], P('dp'), may hold values from 0 to 16, as said below
- prev_scores: bfloat16 [24, 12, 512, 512], P('dp', 'tensor'), may hold values from -6 to 6
- out_grad: bfloat16 [12288, 768], P('dp'), may hold values from -6 to 6
- attn_in_master: float32 [3, 768, 768], P(None, 'dp', 'tensor'), may hold values from -0.21875 to 0.21875
- attn_out_master: float32 [768, 768], P('tensor', 'dp'), may hold values from -0.875 to 0.875
- ffn_in_master: float32 [768, 3072], P('dp', 'tensor'), may hold values from -0.21875 to 0.21875
- ffn_out_master: float32 [3072, 768], P('tensor', 'dp'), may hold values from -0.109375 to 0.109375
- attn_in_first: float32 [3, 768, 768], P(None, 'dp', 'tensor'), may hold values from -0.0024414062 to 0.0024414062
- attn_out_first: float32 [768, 768], P('tensor', 'dp'), may hold values from -0.0024414062 to 0.0024414062
- ffn_in_first: float32 [768, 3072], P('dp', 'tensor'), may hold values from -0.0024414062 to 0.0024414062
- ffn_out_first: float32 [3072, 768], P('tensor', 'dp'), may hold values from -0.0024414062 to 0.0024414062
- attn_in_second: float32 [3, 768, 768], P(None, 'dp', 'tensor'), may hold values from 1.4110135e-07 to 5.644054e-07
- attn_out_second: float32 [768, 768], P('tensor', 'dp'), may hold values from 1.4110135e-07 to 5.644054e-07
- ffn_in_second: float32 [768, 3072], P('dp', 'tensor'), may hold values from 1.4110135e-07 to 5.644054e-07
- ffn_out_second: float32 [3072, 768], P('tensor', 'dp'), may hold values from 1.4110135e-07 to 5.644054e-07
- qv_bias: float32 [2, 768], P(None, 'tensor'), may hold values from -1.75 to 1.75
- ffn_bias: float32 [3072], P('tensor'), may hold values from -1.75 to 1.75
- row_params: float32 [6, 768], replicated, may hold values from -0.75 to 1.65, as said below
- qv_bias_first: float32 [2, 768], P(None, 'tensor'), may hold values from -0.009765625 to 0.009765625
- ffn_bias_first: float32 [3072], P('tensor'), may hold values from -0.0024414062 to 0.0024414062
- row_params_first: float32 [6, 768], replicated, may hold values from -0.009765625 to 0.009765625
- qv_bias_second: float32 [2, 768], P(None, 'tensor'), may hold values from 2.2576216e-06 to 9.030487e-06
- ffn_bias_second: float32 [3072], P('tensor'), may hold values from 7.0550676e-08 to 2.822027e-07
- row_params_second: float32 [6, 768], replicated, may hold values from 2.2576216e-06 to 9.030487e-06
Outputs:
- out_tokens: bfloat16 [12288, 768], P('dp')
- tokens_grad: float32 [12288, 768], P('dp')
- scores_grad: float32 [24, 12, 512, 512], P('dp', 'tensor')
- grad_norm: float32 [], replicated
- attn_in_new: float32 [3, 768, 768], P(None, 'dp', 'tensor')
- attn_out_new: float32 [768, 768], P('tensor', 'dp')
- ffn_in_new: float32 [768, 3072], P('dp', 'tensor')
- ffn_out_new: float32 [3072, 768], P('tensor', 'dp')
- attn_in_first_new: float32 [3, 768, 768], P(None, 'dp', 'tensor')
- attn_out_first_new: float32 [768, 768], P('tensor', 'dp')
- ffn_in_first_new: float32 [768, 3072], P('dp', 'tensor')
- ffn_out_first_new: float32 [3072, 768], P('tensor', 'dp')
- attn_in_second_new: float32 [3, 768, 768], P(None, 'dp', 'tensor')
- attn_out_second_new: float32 [768, 768], P('tensor', 'dp')
- ffn_in_second_new: float32 [768, 3072], P('dp', 'tensor')
- ffn_out_second_new: float32 [3072, 768], P('tensor', 'dp')
- attn_in_copy: bfloat16 [3, 768, 768], P(None, 'dp', 'tensor')
- attn_out_copy: bfloat16 [768, 768], P('tensor', 'dp')
- ffn_in_copy: bfloat16 [768, 3072], P('dp', 'tensor')
- ffn_out_copy: bfloat16 [3072, 768], P('tensor', 'dp')
- qv_bias_new: float32 [2, 768], P(None, 'tensor')
- ffn_bias_new: float32 [3072], P('tensor')
- row_params_new: float32 [6, 768], replicated
- qv_bias_first_new: float32 [2, 768], P(None, 'tensor')
- ffn_bias_first_new: float32 [3072], P('tensor')
- row_params_first_new: float32 [6, 768], replicated
- qv_bias_second_new: float32 [2, 768], P(None, 'tensor')
- ffn_bias_second_new: float32 [3072], P('tensor')
- row_params_second_new: float32 [6, 768], replicated
Inputs may be any that keep to these rules, and one draw needn't show every extreme that they name: `segment_ids`: in each pack, live slots come first and empty slots (0) last; live ids start at 1 and rise by one from one sequence to the next; sequences start at multiples of 32 slots; a pack holds 128, 256, 384 or 512 live slots; the first pack holds one sequence of 512 slots, the second pack 3 * 128 live slots, the last pack 16 sequences of 32 slots. `row_params`: rows 0 and 1 lie between 0.35 and 1.65.
All inputs are finite; a program needn't handle non-finite values.
Results may differ from a plain program's by a relative error of at most 0.012.
The roundings to bfloat16 on the way count: a program that leaves them out, or rounds other values in their place, can miss the bound.
Values may be sent and summed in bfloat16 or wider, within the bound.
A program may use at most 128 MiB of HBM per device.

v0:
```python
from functools import partial
import jax
import jax.numpy as jnp
from jax import lax
from jax.sharding import PartitionSpec as P

D = 768
STEP = 5
beta_one = 0.5
beta_two = 0.5
weight_decay = 0.01
adam_eps = 1e-08
norm_eps = 1e-06
small_rate = 0.5


def layer_norm(rows_in, gain_row, shift_row):
    row_mean = jnp.mean(rows_in, axis=-1, keepdims=True)
    centred = rows_in - row_mean
    spread = jnp.mean(centred * centred, axis=-1, keepdims=True)
    return centred * lax.rsqrt(spread + norm_eps) * gain_row + shift_row


def masked_scores(scale, query_heads, key_heads, prev_block, seg_ids):
    same_seq = seg_ids[:, None] == seg_ids[None, :]
    scores = jnp.einsum(
        "qhe,khe->hqk", query_heads, key_heads, preferred_element_type=jnp.float32
    ) * scale + prev_block.astype(jnp.float32)
    return jnp.where(same_seq[None], scores, -1000000000.0)


def attend(scale, pieces):
    query_heads, key_heads, value_heads, prev_block, seg_ids = pieces
    scores = masked_scores(scale, query_heads, key_heads, prev_block, seg_ids)
    row_top = jnp.max(scores, axis=-1, keepdims=True)
    expo = jnp.exp(scores - row_top)
    row_total = jnp.sum(expo, axis=-1, keepdims=True)
    weights_low = (expo / row_total).astype(jnp.bfloat16)
    context_heads = jnp.einsum(
        "hqk,khe->qhe", weights_low, value_heads, preferred_element_type=jnp.float32
    )
    return (context_heads.astype(jnp.bfloat16), row_top + jnp.log(row_total))


def attend_back(scale, pieces):
    query_heads, key_heads, value_heads, prev_block, seg_ids, row_lse, grad_heads = pieces
    scores = masked_scores(scale, query_heads, key_heads, prev_block, seg_ids)
    soft = jnp.exp(scores - row_lse)
    soft_low = soft.astype(jnp.bfloat16)
    grad_soft = jnp.einsum(
        "qhe,khe->hqk", grad_heads, value_heads, preferred_element_type=jnp.float32
    )
    row_dot = jnp.sum(soft * grad_soft, axis=-1, keepdims=True)
    score_grad = (soft * (grad_soft - row_dot)).astype(jnp.bfloat16)
    grad_query = (
        jnp.einsum("hqk,khe->qhe", score_grad, key_heads, preferred_element_type=jnp.float32)
        * scale
    ).astype(jnp.bfloat16)
    grad_key = (
        jnp.einsum("hqk,qhe->khe", score_grad, query_heads, preferred_element_type=jnp.float32)
        * scale
    ).astype(jnp.bfloat16)
    grad_value = jnp.einsum(
        "hqk,qhe->khe", soft_low, grad_heads, preferred_element_type=jnp.float32
    ).astype(jnp.bfloat16)
    return (grad_query, grad_key, grad_value, score_grad.astype(jnp.float32))


def adam_update(weight, gradient, first_moment, second_moment, decay_rate, learn_rate):
    first_new = beta_one * first_moment + (1.0 - beta_one) * gradient
    second_new = beta_two * second_moment + (1.0 - beta_two) * gradient * gradient
    corrected = (
        first_new
        / (1.0 - beta_one**STEP)
        / (jnp.sqrt(second_new / (1.0 - beta_two**STEP)) + adam_eps)
    )
    return (weight - learn_rate * (corrected + decay_rate * weight), first_new, second_new)


def on_device(
    tokens,
    segment_ids,
    prev_scores,
    out_grad,
    attn_in_master,
    attn_out_master,
    ffn_in_master,
    ffn_out_master,
    attn_in_first,
    attn_out_first,
    ffn_in_first,
    ffn_out_first,
    attn_in_second,
    attn_out_second,
    ffn_in_second,
    ffn_out_second,
    qv_bias,
    ffn_bias,
    row_params,
    qv_bias_first,
    ffn_bias_first,
    row_params_first,
    qv_bias_second,
    ffn_bias_second,
    row_params_second,
):
    attn_in, attn_out, ffn_in, ffn_out = (
        lax.all_gather(attn_in_master.astype(jnp.bfloat16), "dp", axis=1, tiled=True),
        lax.all_gather(attn_out_master.astype(jnp.bfloat16), "dp", axis=1, tiled=True),
        lax.all_gather(ffn_in_master.astype(jnp.bfloat16), "dp", axis=0, tiled=True),
        lax.all_gather(ffn_out_master.astype(jnp.bfloat16), "dp", axis=1, tiled=True),
    )
    pack_count, pack_len = segment_ids.shape
    head_count = prev_scores.shape[1]
    head_width = attn_in.shape[2] // head_count
    scale = head_width ** (-0.5)
    token_count = tokens.shape[0]
    dp_count = lax.axis_size("dp")
    tensor_count = lax.axis_size("tensor")

    def split_heads(matrix):
        return matrix.reshape(pack_count, pack_len, head_count, head_width)

    projected = jnp.einsum("td,cde->cte", tokens, attn_in, preferred_element_type=jnp.float32)
    query_rows = (projected[0] + qv_bias[0]).astype(jnp.bfloat16)
    key_rows = projected[1].astype(jnp.bfloat16)
    value_rows = (projected[2] + qv_bias[1]).astype(jnp.bfloat16)
    query_heads = split_heads(query_rows)
    key_heads = split_heads(key_rows)
    value_heads = split_heads(value_rows)
    context_heads, row_lse = lax.map(
        partial(attend, scale), (query_heads, key_heads, value_heads, prev_scores, segment_ids)
    )
    context = context_heads.reshape(token_count, -1)
    attn_partial = jnp.dot(context, attn_out, preferred_element_type=jnp.float32)
    live_whole = (segment_ids > 0).astype(jnp.float32).reshape(token_count, 1)
    rows_start = tokens.astype(jnp.float32)
    attended = lax.psum(attn_partial, "tensor") + row_params[2]
    cotangent = out_grad.astype(jnp.float32)
    residual_one = rows_start + attended
    normed, first_pull = jax.vjp(layer_norm, residual_one, row_params[0], row_params[3])
    normed_low = normed.astype(jnp.bfloat16)
    pre_act = jnp.dot(normed_low, ffn_in, preferred_element_type=jnp.float32) + ffn_bias
    activation, gelu_pull = jax.vjp(partial(jax.nn.gelu, approximate=False), pre_act)
    act_low = activation.astype(jnp.bfloat16)
    ffn_partial = jnp.dot(act_low, ffn_out, preferred_element_type=jnp.float32)
    ffn_output = lax.psum(ffn_partial, "tensor") + row_params[4]

    def final_norm(rows_in, gain_row, shift_row):
        return layer_norm(rows_in, gain_row, shift_row) * live_whole

    final_rows, second_pull = jax.vjp(final_norm, normed + ffn_output, row_params[1], row_params[5])
    final_low = final_rows.astype(jnp.bfloat16)
    grad_res_two, grad_gain_two, grad_shift_two = second_pull(cotangent)
    grad_ffn_low = grad_res_two.astype(jnp.bfloat16)
    grad_ffn_out_bias = jnp.sum(grad_ffn_low.astype(jnp.float32), axis=0)
    grad_ffn_out = jnp.einsum(
        "tf,td->fd", act_low, grad_ffn_low, preferred_element_type=jnp.float32
    )
    grad_act = jnp.einsum("td,fd->tf", grad_ffn_low, ffn_out, preferred_element_type=jnp.float32)
    (grad_pre,) = gelu_pull(grad_act)
    grad_pre_low = grad_pre.astype(jnp.bfloat16)
    grad_ffn_bias = jnp.sum(grad_pre_low.astype(jnp.float32), axis=0)
    grad_ffn_in = jnp.einsum(
        "td,tf->df", normed_low, grad_pre_low, preferred_element_type=jnp.float32
    )
    hidden_part = jnp.einsum("tf,df->td", grad_pre_low, ffn_in, preferred_element_type=jnp.float32)
    grad_normed = grad_res_two + lax.psum(hidden_part, "tensor")
    grad_res_one, grad_gain_one, grad_shift_one = first_pull(grad_normed)
    att_low = grad_res_one.astype(jnp.bfloat16)
    grad_att_bias = jnp.sum(att_low.astype(jnp.float32), axis=0)
    grad_attn_out = jnp.einsum("te,td->ed", context, att_low, preferred_element_type=jnp.float32)
    grad_context = jnp.einsum(
        "td,ed->te", att_low, attn_out, preferred_element_type=jnp.float32
    ).astype(jnp.bfloat16)
    grad_query, grad_key, grad_value, scores_grad = lax.map(
        partial(attend_back, scale),
        (
            query_heads,
            key_heads,
            value_heads,
            prev_scores,
            segment_ids,
            row_lse,
            split_heads(grad_context),
        ),
    )
    grad_proj = jnp.stack(
        [
            grad_query.reshape(token_count, -1),
            grad_key.reshape(token_count, -1),
            grad_value.reshape(token_count, -1),
        ]
    )
    grad_attn_in = jnp.einsum("td,cte->cde", tokens, grad_proj, preferred_element_type=jnp.float32)
    grad_qv_bias = jnp.stack(
        [
            jnp.sum(grad_proj[0].astype(jnp.float32), axis=0),
            jnp.sum(grad_proj[2].astype(jnp.float32), axis=0),
        ]
    )
    input_part = jnp.einsum("cte,cde->td", grad_proj, attn_in, preferred_element_type=jnp.float32)
    norm_stack = jnp.stack([grad_gain_one, grad_gain_two, grad_shift_one, grad_shift_two])
    tokens_grad = grad_res_one + lax.psum(input_part, "tensor")
    grad_rows = jnp.stack(
        [
            norm_stack[0],
            norm_stack[1],
            grad_att_bias,
            norm_stack[2],
            grad_ffn_out_bias,
            norm_stack[3],
        ]
    )
    summed = lax.psum(
        (
            grad_attn_in,
            grad_attn_out,
            grad_ffn_in,
            grad_ffn_out,
            grad_qv_bias,
            grad_ffn_bias,
            grad_rows,
        ),
        "dp",
    )
    dp_index = lax.axis_index("dp")

    def own_part(whole_grad, shard, along):
        extent = shard.shape[along]
        return lax.dynamic_slice_in_dim(whole_grad, dp_index * extent, extent, along)

    shares = (
        own_part(summed[0], attn_in_master, 1),
        own_part(summed[1], attn_out_master, 1),
        own_part(summed[2], ffn_in_master, 0),
        own_part(summed[3], ffn_out_master, 1),
    )
    small_sums = (summed[4], summed[5], summed[6])
    local_squares = jnp.float32(0.0)
    for share in shares:
        local_squares = local_squares + jnp.sum(share * share)
    local_squares = (
        local_squares
        + (jnp.sum(small_sums[0] * small_sums[0]) + jnp.sum(small_sums[1] * small_sums[1]))
        / dp_count
    )
    local_squares = local_squares + jnp.sum(small_sums[2] * small_sums[2]) / (
        dp_count * tensor_count
    )
    total_squares = lax.psum(local_squares, ("dp", "tensor"))
    grad_norm = jnp.sqrt(total_squares)
    factor = 1.0 / jnp.maximum(grad_norm, 1.0)
    olds = (
        attn_in_master,
        attn_out_master,
        ffn_in_master,
        ffn_out_master,
        qv_bias,
        ffn_bias,
        row_params,
    )
    firsts = (
        attn_in_first,
        attn_out_first,
        ffn_in_first,
        ffn_out_first,
        qv_bias_first,
        ffn_bias_first,
        row_params_first,
    )
    seconds = (
        attn_in_second,
        attn_out_second,
        ffn_in_second,
        ffn_out_second,
        qv_bias_second,
        ffn_bias_second,
        row_params_second,
    )
    gradients = (
        shares[0],
        shares[1],
        shares[2],
        shares[3],
        small_sums[0],
        small_sums[1],
        small_sums[2],
    )
    decays = (weight_decay, weight_decay, weight_decay, weight_decay, 0.0, 0.0, 0.0)
    big_rate = D ** (-0.5)
    rates = (big_rate, big_rate, big_rate, big_rate, small_rate, small_rate, small_rate)
    updated = [
        adam_update(
            olds[place],
            gradients[place] * factor,
            firsts[place],
            seconds[place],
            decays[place],
            rates[place],
        )
        for place in range(7)
    ]
    return (
        final_low,
        tokens_grad,
        scores_grad,
        grad_norm,
        updated[0][0],
        updated[1][0],
        updated[2][0],
        updated[3][0],
        updated[0][1],
        updated[1][1],
        updated[2][1],
        updated[3][1],
        updated[0][2],
        updated[1][2],
        updated[2][2],
        updated[3][2],
        updated[0][0].astype(jnp.bfloat16),
        updated[1][0].astype(jnp.bfloat16),
        updated[2][0].astype(jnp.bfloat16),
        updated[3][0].astype(jnp.bfloat16),
        updated[4][0],
        updated[5][0],
        updated[6][0],
        updated[4][1],
        updated[5][1],
        updated[6][1],
        updated[4][2],
        updated[5][2],
        updated[6][2],
    )


def solution(mesh):
    in_specs = (
        P("dp", None),
        P("dp", None),
        P("dp", "tensor", None, None),
        P("dp", None),
        P(None, "dp", "tensor"),
        P("tensor", "dp"),
        P("dp", "tensor"),
        P("tensor", "dp"),
        P(None, "dp", "tensor"),
        P("tensor", "dp"),
        P("dp", "tensor"),
        P("tensor", "dp"),
        P(None, "dp", "tensor"),
        P("tensor", "dp"),
        P("dp", "tensor"),
        P("tensor", "dp"),
        P(None, "tensor"),
        P("tensor"),
        P(),
        P(None, "tensor"),
        P("tensor"),
        P(),
        P(None, "tensor"),
        P("tensor"),
        P(),
    )
    out_specs = (
        P("dp", None),
        P("dp", None),
        P("dp", "tensor", None, None),
        P(),
        P(None, "dp", "tensor"),
        P("tensor", "dp"),
        P("dp", "tensor"),
        P("tensor", "dp"),
        P(None, "dp", "tensor"),
        P("tensor", "dp"),
        P("dp", "tensor"),
        P("tensor", "dp"),
        P(None, "dp", "tensor"),
        P("tensor", "dp"),
        P("dp", "tensor"),
        P("tensor", "dp"),
        P(None, "dp", "tensor"),
        P("tensor", "dp"),
        P("dp", "tensor"),
        P("tensor", "dp"),
        P(None, "tensor"),
        P("tensor"),
        P(),
        P(None, "tensor"),
        P("tensor"),
        P(),
        P(None, "tensor"),
        P("tensor"),
        P(),
    )
    return jax.shard_map(
        on_device, mesh=mesh, in_specs=in_specs, out_specs=out_specs, check_vma=False
    )
```

profile of v0, /device:TPU:0, one launch (start us, length us, event | category | flops | bytes accessed | tf_op | source)
XLA Modules:
  0.0 938.5 jit_solution(11996233657050409264)
XLA Ops:
  9.2 38.6 %all_gather.12 = bf16[3,768,192]{2,0,1:T(4,128)(2,1)S(1)} all-gather(bf16[3,96,192]{2,0,1:T(4,128)(2,1)S(1)} %copy.141), channel_id=1, replica_groups=mesh['dp'=8,'tensor'=4] {'dp'}, dimensions={1}, use_global_device_ids=true | all-gather | bytes 995328 | tf_op jit(solution)/shard_map/all_gather | solution.py:108
  47.8 4.4 convolution_bitcast_fusion.1
  60.5 6.6 copy.146
  67.2 14.8 %while.28 = (s32[]{:T(128)}, bf16[3,512,3,64]{1,3,2,0:T(8,128)(2,1)S(1)}, f32[3,3,512,1]{2,1,3,0:T(4,128)S(1)}, bf16[3,512,3,64]{1,3,2,0:T(8,128)(2,1)}, s32[3,5...) while((s32[]{:T(128)}, ...), condition=%wide.region_3.4_spmd, body=%wide.region_0.3_spmd.sunk | while | flops 209549824 | bytes 12388973 | solution.py:131
  82.7 31.0 %all_gather.13 = bf16[192,768]{0,1:T(8,128)(2,1)S(1)} all-gather(bf16[192,96]{0,1:T(8,128)(2,1)S(1)} %copy.148), channel_id=1, replica_groups=mesh['dp'=8,'tensor'=4] {'dp'}, dimensions={1}, use_global_device_ids=true | all-gather | bytes 331776 | tf_op jit(solution)/shard_map/all_gather | solution.py:109
  120.5 89.9 %all-reduce.8.cloned.1.call-done = f32[1536,768]{1,0:T(8,128)} async-done(((f32[1536,768]{1,0:T(8,128)}), f32[1536,768]{1,0:T(8,128)}) %all-reduce.8.cloned.1.call-update) | async-done | bytes 4718608 | tf_op jit(solution)/shard_map/psum | solution.py:138
  216.7 14.5 %multiply_convert_fusion.2 = (bf16[1536,768]{1,0:T(8,128)(2,1)}, f32[1536,768]{1,0:T(8,128)}, f32[1536,768]{1,0:T(8,128)}) fusion(f32[768]{0:T(1024)S(1)} %copy-done.28, bf16[1536,768]{1,0:T(8,128)(2,1)S(1)} %fusion.62, bf16[768,768]{1,0:T(8,128)(2,1)} %all-gather.3.cloned.1.call-done), kind=kOutput, calls=%fused_computation.82 | convolution fusion | flops 1889796096 | bytes 15338496 | tf_op jit(solution)/shard_map/dot_general | solution.py:143
  231.2 6.2 fusion.99
  237.7 94.0 %all-reduce.10.cloned.1.call-done = f32[1536,768]{1,0:T(8,128)} async-done(((f32[1536,768]{1,0:T(8,128)}), f32[1536,768]{1,0:T(8,128)}) %all-reduce.10.cloned.1.call-update) | async-done | bytes 4718608 | tf_op jit(solution)/shard_map/psum | solution.py:147
  331.7 4.7 fusion.93
  340.4 3.8 fusion.92
  351.8 4.2 fusion.100
  356.1 5.3 fusion.102
  365.0 85.4 %all-reduce.12.cloned.1.call-done = f32[1536,768]{1,0:T(8,128)} async-done(((f32[1536,768]{1,0:T(8,128)}), f32[1536,768]{1,0:T(8,128)}) %all-reduce.12.cloned.1.call-update) | async-done | bytes 4718608 | tf_op jit(solution)/shard_map/psum | solution.py:168
  450.3 6.7 multiply_reduce_fusion.2
  457.1 3.8 fusion.91
  468.6 55.0 %while.29 = (s32[]{:T(128)}, bf16[3,512,3,64]{1,3,2,0:T(8,128)(2,1)}, bf16[3,512,3,64]{1,3,2,0:T(8,128)(2,1)}, bf16[3,512,3,64]{1,3,2,0:T(8,128)(2,1)}, f32[3,3,...) while((s32[]{:T(128)}, ...), condition=%wide.region_17.18_spmd, body=%wide.region_15.17_spmd.sunk | while | flops 513505792 | bytes 43427472 | solution.py:176
  533.6 4.9 fusion.66
  540.5 4.5 convolution_bitcast_fusion
  548.2 39.3 %all-reduce = (f32[2,192]{1,0:T(2,128)S(1)}, f32[768]{0:T(1024)S(1)}, f32[6,768]{1,0:T(8,128)S(1)}) all-reduce(f32[2,192]{1,0:T(2,128)S(1)} %pad_maximum_fusion, f32[768]{0:T(1024)S(1)} %get-tuple-element.431, f32[6,768]{1,0:T(8,128)S(1)} %stack.31), channel_id=1, replica_groups=mesh['dp'=8,'tensor'=4] {'dp'}, use_global_device_ids=true, to_apply=%region_29.30 | all-reduce | flops 5760 | bytes 46080 | tf_op jit(solution)/shard_map/psum | solution.py:215
  591.2 183.0 %all-reduce.16.cloned.1.call-done = (f32[3,768,192]{1,2,0:T(8,128)}, f32[192,768]{1,0:T(8,128)}, f32[768,768]{1,0:T(8,128)}, f32[768,768]{0,1:T(8,128)}) async-done(((f32[3,768,192]{1,2,0:T(8,128)}, f32[192,768]{1,0:T(8,128)}, f32[768,768]{1,0:T(8,128)}, f32[768,768]{0,1:T(8,128)}), (f32[3,768,192]{1,2,0:T(8,128)}, f32[192,768]{1,0:T(8,128)}, f32[768,768]{1,0:T(8,128)}, ...) | async-done | bytes 7077904 | tf_op jit(solution)/shard_map/psum | solution.py:215
  783.6 86.5 %all-reduce.14.cloned.1.call-done = f32[1536,768]{1,0:T(8,128)} async-done(((f32[1536,768]{1,0:T(8,128)}), f32[1536,768]{1,0:T(8,128)}) %all-reduce.14.cloned.1.call-update) | async-done | bytes 4718608 | tf_op jit(solution)/shard_map/psum | solution.py:204
  870.1 6.5 add_add_fusion.4
  876.6 39.5 %psum.95 = f32[]{:T(128)} all-reduce(f32[]{:T(128)S(6)} %add.314), channel_id=1, replica_groups=mesh['dp'=8,'tensor'=4] {'dp','tensor'}, use_global_device_ids=true, to_apply=%region_42.43 | all-reduce | flops 1 | bytes 8 | tf_op jit(solution)/shard_map/psum | solution.py:251
  (241 shorter events, 152.1 us)
Async XLA Ops:
  8.0 202.4 %all-reduce.8.cloned.1.call-start = ((), (), s32[]{:S(2)}) async-start(), calls=%async_computation | async-start | bytes 9437184 | tf_op jit(solution)/shard_map/psum | solution.py:138
  67.2 15.5 %copy-start.13 = (f32[192,96]{1,0:T(8,128)S(1)}, f32[192,96]{1,0:T(8,128)}, u32[]{:S(2)}) copy-start(f32[192,96]{1,0:T(8,128)} %param.34) | copy-start | bytes 221188
  113.7 6.7 copy-start.22
  113.7 96.7 %copy-start.5 = (bf16[1536,768]{1,0:T(8,128)(2,1)S(1)}, bf16[1536,768]{1,0:T(8,128)(2,1)}, u32[]{:S(2)}) copy-start(bf16[1536,768]{1,0:T(8,128)(2,1)} %param.29) | copy-start | bytes 7077892
  116.8 99.9 %all-gather.3.cloned.1.call-start = ((), (), s32[]{:S(2)}) async-start(), calls=%async_computation.1 | async-start | bytes 1327104 | tf_op jit(solution)/shard_map/all_gather | solution.py:110
  118.5 112.7 %all-gather.5.cloned.1.call-start = ((), (), s32[]{:S(2)}) async-start(), calls=%async_computation.2 | async-start | bytes 1327104 | tf_op jit(solution)/shard_map/all_gather | solution.py:111
  120.2 211.5 %all-reduce.10.cloned.1.call-start = ((), (), s32[]{:S(2)}) async-start(), calls=%async_computation.3 | async-start | bytes 9437184 | tf_op jit(solution)/shard_map/psum | solution.py:147
  237.4 213.0 %all-reduce.12.cloned.1.call-start = ((), (), s32[]{:S(2)}) async-start(), calls=%async_computation.4 | async-start | bytes 9437184 | tf_op jit(solution)/shard_map/psum | solution.py:168
  356.0 418.2 %all-reduce.16.cloned.1.call-start = ((), (), s32[]{:S(2)}) async-start(), calls=%async_computation.6 | async-start | bytes 14155776 | tf_op jit(solution)/shard_map/psum | solution.py:215
  538.6 331.5 %all-reduce.14.cloned.1.call-start = ((), (), s32[]{:S(2)}) async-start(), calls=%async_computation.5 | async-start | bytes 9437184 | tf_op jit(solution)/shard_map/psum | solution.py:204
  783.6 138.2 %copy-start.14 = (f32[192,96]{1,0:T(8,128)S(1)}, f32[192,96]{1,0:T(8,128)}, u32[]{:S(2)}) copy-start(f32[192,96]{1,0:T(8,128)} %param.34) | copy-start | bytes 221188
  876.6 47.1 %copy-start.11 = (f32[96,768]{1,0:T(8,128)S(1)}, f32[96,768]{1,0:T(8,128)}, u32[]{:S(2)}) copy-start(f32[96,768]{1,0:T(8,128)} %param.35) | copy-start | bytes 884740
  876.6 47.1 %copy-start.17 = (f32[96,768]{1,0:T(8,128)S(1)}, f32[96,768]{1,0:T(8,128)}, u32[]{:S(2)}) copy-start(f32[96,768]{1,0:T(8,128)} %param.39) | copy-start | bytes 884740
  876.6 47.1 %copy-start.18 = (f32[96,768]{1,0:T(8,128)S(1)}, f32[96,768]{1,0:T(8,128)}, u32[]{:S(2)}) copy-start(f32[96,768]{1,0:T(8,128)} %param.43) | copy-start | bytes 884740
  876.6 49.2 %copy-start.12 = (f32[768,96]{0,1:T(8,128)S(1)}, f32[768,96]{0,1:T(8,128)}, u32[]{:S(2)}) copy-start(f32[768,96]{0,1:T(8,128)} %param.36) | copy-start | bytes 884740
  876.6 49.2 %copy-start.19 = (f32[768,96]{0,1:T(8,128)S(1)}, f32[768,96]{0,1:T(8,128)}, u32[]{:S(2)}) copy-start(f32[768,96]{0,1:T(8,128)} %param.40) | copy-start | bytes 884740
  916.9 11.1 %copy-start.27 = (f32[2,192]{1,0:T(2,128)S(1)}, f32[2,192]{1,0:T(2,128)}, u32[]{:S(2)}) copy-start(f32[2,192]{1,0:T(2,128)} %param.45) | copy-start | bytes 4612
  916.9 12.3 %copy-start.23 = (f32[6,768]{1,0:T(8,128)S(1)}, f32[6,768]{1,0:T(8,128)}, u32[]{:S(2)}) copy-start(f32[6,768]{1,0:T(8,128)} %param.47) | copy-start | bytes 55300
  918.3 9.6 %copy-start.31 = (f32[2,192]{1,0:T(2,128)S(1)}, f32[2,192]{1,0:T(2,128)}, u32[]{:S(2)}) copy-start(f32[2,192]{1,0:T(2,128)} %param.48) | copy-start | bytes 4612
  918.3 9.6 %copy-start.32 = (f32[2,192]{1,0:T(2,128)S(1)}, f32[2,192]{1,0:T(2,128)}, u32[]{:S(2)}) copy-start(f32[2,192]{1,0:T(2,128)} %param.51) | copy-start | bytes 4612
  918.3 10.2 %copy-start.29 = (f32[768]{0:T(1024)S(1)}, f32[768]{0:T(1024)}, u32[]{:S(2)}) copy-start(f32[768]{0:T(1024)} %param.49) | copy-start | bytes 9220
  918.3 10.2 %copy-start.30 = (f32[768]{0:T(1024)S(1)}, f32[768]{0:T(1024)}, u32[]{:S(2)}) copy-start(f32[768]{0:T(1024)} %param.52) | copy-start | bytes 9220
  918.3 10.8 %copy-start.24 = (f32[6,768]{1,0:T(8,128)S(1)}, f32[6,768]{1,0:T(8,128)}, u32[]{:S(2)}) copy-start(f32[6,768]{1,0:T(8,128)} %param.50) | copy-start | bytes 55300
  918.3 10.8 %copy-start.25 = (f32[6,768]{1,0:T(8,128)S(1)}, f32[6,768]{1,0:T(8,128)}, u32[]{:S(2)}) copy-start(f32[6,768]{1,0:T(8,128)} %param.53) | copy-start | bytes 55300
  (23 other events, 80.8 us)
Sparse Core Ops, SparseCore 0:
  116.9 93.4 all-reduce.7
  237.5 94.1 all-reduce.9
  356.1 94.1 all-reduce.11
Sparse Core Ops, SparseCore 1:
  120.0 40.8 all-gather.2
  163.5 39.9 all-gather.4
  538.6 235.5 all-reduce.15
  777.3 92.7 all-reduce.13
where the time goes:
time: 947 us; the launch traced here: 938 us
  waiting for transfers between devices  539 us (57%)
  blocking collectives  148 us (16%)
  matrix products  102 us (11%)
  other arithmetic  69.2 us (7%)
  local copies, waits for them, and re-layouts  56 us (6%)
  between operations  22.9 us (2%)
    psum x1, waiting for transfers between devices, on_device(): lax.psum((grad_attn_in, grad_attn_out, grad_ffn_in, grad_ffn_out, grad_qv...  183 us
    psum x1, waiting for transfers between devices, on_device(): ffn_output = lax.psum(ffn_partial, 'tensor') + row_params[4]  94 us
    psum x1, waiting for transfers between devices, on_device(): attended = lax.psum(attn_partial, 'tensor') + row_params[2]  89.9 us
    psum x1, waiting for transfers between devices, on_device(): tokens_grad = grad_res_one + lax.psum(input_part, 'tensor')  86.5 us
    psum x1, waiting for transfers between devices, on_device(): grad_normed = grad_res_two + lax.psum(hidden_part, 'tensor')  85.4 us
    psum x1, blocking collectives, on_device(): total_squares = lax.psum(local_squares, ('dp', 'tensor'))  39.5 us
    psum x1, blocking collectives, on_device(): lax.psum((grad_attn_in, grad_attn_out, grad_ffn_in, grad_ffn_out, grad_qv...  39.3 us
    all_gather x1, blocking collectives, on_device(): lax.all_gather(attn_in_master.astype(jnp.bfloat16), 'dp', axis=1, tiled=T...  38.6 us
  transfers between devices with their start and end apart: 7, of which 5 were waited for; matrix products, arithmetic and copies ran while one was open for 5% of the time, Pallas kernels for 0%

commit v1 on v0

--- a/solution.py
+++ b/solution.py
@@ -201,7 +201,7 @@
     )
     input_part = jnp.einsum("cte,cde->td", grad_proj, attn_in, preferred_element_type=jnp.float32)
     norm_stack = jnp.stack([grad_gain_one, grad_gain_two, grad_shift_one, grad_shift_two])
-    tokens_grad = grad_res_one + lax.psum(input_part, "tensor")
+    tokens_grad = grad_res_one + jnp.sum(lax.all_gather(input_part, "tensor"), axis=0)
     grad_rows = jnp.stack(
         [
             norm_stack[0],

time: 947 us -> 859 us (0.907)
  waiting for transfers between devices: 539 us -> 454 us
  matrix products: 102 us -> 88.7 us
  other arithmetic: 69.2 us -> 81.5 us
    psum x1 -> x0, waiting for transfers between devices: 86.5 us -> none  [on_device(): tokens_grad = grad_res_one + lax.psum(input_part, 'tensor')]
    reduce_sum x0 -> x1, other arithmetic: none -> 10.4 us  [on_device(): jnp.sum(lax.all_gather(input_part, 'tensor'), axis=0)]
  transfers between devices with their start and end apart: 7 -> 7, of which waited for: 5 -> 4; matrix products, arithmetic and copies ran while one was open for 5% -> 7% of each run, Pallas kernels for 0% -> 0%
where the time goes in v1:
time: 859 us; the launch traced here: 851 us
  waiting for transfers between devices  454 us (53%)
  blocking collectives  150 us (17%)
  matrix products  88.7 us (10%)
  other arithmetic  81.5 us (9%)
  local copies, waits for them, and re-layouts  53.4 us (6%)
  between operations  22.9 us (3%)
    psum x1, waiting for transfers between devices, on_device(): lax.psum((grad_attn_in, grad_attn_out, grad_ffn_in, grad_ffn_out, grad_qv...  183 us
    psum x1, waiting for transfers between devices, on_device(): ffn_output = lax.psum(ffn_partial, 'tensor') + row_params[4]  94 us
    psum x1, waiting for transfers between devices, on_device(): attended = lax.psum(attn_partial, 'tensor') + row_params[2]  91.7 us
    psum x1, waiting for transfers between devices, on_device(): grad_normed = grad_res_two + lax.psum(hidden_part, 'tensor')  84.5 us
    psum x1, blocking collectives, on_device(): lax.psum((grad_attn_in, grad_attn_out, grad_ffn_in, grad_ffn_out, grad_qv...  39.4 us
    psum x1, blocking collectives, on_device(): total_squares = lax.psum(local_squares, ('dp', 'tensor'))  39 us
    all_gather x1, blocking collectives, on_device(): lax.all_gather(attn_in_master.astype(jnp.bfloat16), 'dp', axis=1, tiled=T...  38.6 us
    all_gather x1, blocking collectives, on_device(): lax.all_gather(attn_out_master.astype(jnp.bfloat16), 'dp', axis=1, tiled=...  33 us
  transfers between devices with their start and end apart: 7, of which 4 were waited for; matrix products, arithmetic and copies ran while one was open for 7% of the time, Pallas kernels for 0%

profile of v1, /device:TPU:0, one launch (start us, length us, event | category | flops | bytes accessed | tf_op | source)
XLA Modules:
  0.0 851.1 jit_solution(1842483922507633566)
XLA Ops:
  9.2 38.6 %all_gather.18 = bf16[3,768,192]{2,0,1:T(4,128)(2,1)S(1)} all-gather(bf16[3,96,192]{2,0,1:T(4,128)(2,1)S(1)} %copy.141), channel_id=1, replica_groups=mesh['dp'=8,'tensor'=4] {'dp'}, dimensions={1}, use_global_device_ids=true | all-gather | bytes 995328 | tf_op jit(solution)/shard_map/all_gather | solution.py:108
  47.8 4.4 convolution_bitcast_fusion.1
  53.7 33.0 %all_gather.19 = bf16[192,768]{0,1:T(8,128)(2,1)} all-gather(bf16[192,96]{0,1:T(8,128)(2,1)S(1)} %copy.148), channel_id=1, replica_groups=mesh['dp'=8,'tensor'=4] {'dp'}, dimensions={1}, use_global_device_ids=true | all-gather | bytes 331776 | tf_op jit(solution)/shard_map/all_gather | solution.py:109
  91.2 6.6 copy.146
  97.9 11.3 %while.28 = (s32[]{:T(128)}, bf16[3,512,3,64]{1,3,2,0:T(8,128)(2,1)S(1)}, f32[3,3,512,1]{2,1,3,0:T(4,128)S(1)}, bf16[3,512,3,64]{1,3,2,0:T(8,128)(2,1)S(1)}, s32...) while((s32[]{:T(128)}, ...), condition=%wide.region_3.4_spmd, body=%wide.region_0.3_spmd.sunk | while | flops 209549824 | bytes 12388973 | solution.py:131
  114.8 91.7 %all-reduce.7.cloned.1.call-done = f32[1536,768]{1,0:T(8,128)} async-done(((f32[1536,768]{1,0:T(8,128)}), f32[1536,768]{1,0:T(8,128)}) %all-reduce.7.cloned.1.call-update) | async-done | bytes 4718608 | tf_op jit(solution)/shard_map/psum | solution.py:138
  214.5 15.1 %multiply_convert_fusion.2 = (bf16[1536,768]{1,0:T(8,128)(2,1)}, f32[1536,768]{1,0:T(8,128)}, f32[1536,768]{1,0:T(8,128)}) fusion(f32[768]{0:T(1024)S(1)} %copy-done.33, bf16[1536,768]{1,0:T(8,128)(2,1)} %fusion.62, bf16[768,768]{1,0:T(8,128)(2,1)} %all-gather.5.cloned.1.call-done), kind=kOutput, calls=%fused_computation.82 | convolution fusion | flops 1889796096 | bytes 15338496 | tf_op jit(solution)/shard_map/dot_general | solution.py:143
  229.6 6.2 fusion.99
  236.1 94.0 %all-reduce.9.cloned.1.call-done = f32[1536,768]{1,0:T(8,128)} async-done(((f32[1536,768]{1,0:T(8,128)}), f32[1536,768]{1,0:T(8,128)}) %all-reduce.9.cloned.1.call-update) | async-done | bytes 4718608 | tf_op jit(solution)/shard_map/psum | solution.py:147
  330.1 4.7 fusion.93
  338.8 3.8 fusion.92
  345.4 4.0 convert_reduce_fusion.2
  350.9 4.2 fusion.100
  355.2 6.1 fusion.102
  364.9 84.5 %all-reduce.11.cloned.1.call-done = f32[1536,768]{1,0:T(8,128)} async-done(((f32[1536,768]{1,0:T(8,128)}), f32[1536,768]{1,0:T(8,128)}) %all-reduce.11.cloned.1.call-update) | async-done | bytes 4718608 | tf_op jit(solution)/shard_map/psum | solution.py:168
  449.4 6.7 multiply_reduce_fusion.2
  466.5 46.8 %while.29 = (s32[]{:T(128)}, bf16[3,512,3,64]{1,3,2,0:T(8,128)(2,1)}, bf16[3,512,3,64]{1,3,2,0:T(8,128)(2,1)}, bf16[3,512,3,64]{1,3,2,0:T(8,128)(2,1)}, f32[3,3,...) while((s32[]{:T(128)}, ...), condition=%wide.region_17.18_spmd, body=%wide.region_15.17_spmd.sunk | while | flops 513505792 | bytes 60731108 | solution.py:176
  521.1 4.4 fusion.66
  527.5 4.5 convolution_bitcast_fusion
  534.9 39.4 %all-reduce = (f32[2,192]{1,0:T(2,128)S(1)}, f32[768]{0:T(1024)S(1)}, f32[6,768]{1,0:T(8,128)S(1)}) all-reduce(f32[2,192]{1,0:T(2,128)S(1)} %pad_maximum_fusion, f32[768]{0:T(1024)S(1)} %copy-done.34, f32[6,768]{1,0:T(8,128)S(1)} %stack.31), channel_id=1, replica_groups=mesh['dp'=8,'tensor'=4] {'dp'}, use_global_device_ids=true, to_apply=%region_29.30 | all-reduce | flops 5760 | bytes 46080 | tf_op jit(solution)/shard_map/psum | solution.py:215
  578.0 183.3 %all-reduce.13.cloned.1.call-done = (f32[3,768,192]{1,2,0:T(8,128)}, f32[192,768]{1,0:T(8,128)}, f32[768,768]{1,0:T(8,128)}, f32[768,768]{0,1:T(8,128)}) async-done(((f32[3,768,192]{1,2,0:T(8,128)}, f32[192,768]{1,0:T(8,128)}, f32[768,768]{1,0:T(8,128)}, f32[768,768]{0,1:T(8,128)}), (f32[3,768,192]{1,2,0:T(8,128)}, f32[192,768]{1,0:T(8,128)}, f32[768,768]{1,0:T(8,128)}, ...) | async-done | bytes 7077904 | tf_op jit(solution)/shard_map/psum | solution.py:215
  770.8 39.0 %psum.87 = f32[]{:T(128)} all-reduce(f32[]{:T(128)S(6)} %add.312), channel_id=1, replica_groups=mesh['dp'=8,'tensor'=4] {'dp','tensor'}, use_global_device_ids=true, to_apply=%region_42.43 | all-reduce | flops 1 | bytes 8 | tf_op jit(solution)/shard_map/psum | solution.py:251
  825.6 10.4 %reduce_sum.283 = f32[1536,768]{1,0:T(8,128)} reduce(f32[4,1536,768]{2,1,0:T(8,128)} %bitcast.171, f32[]{:T(128)} %constant.74.clone.1), dimensions={0}, to_apply=%region_18.19 | reduce | flops 3538944 | bytes 23592964 | tf_op jit(solution)/shard_map/reduce_sum | solution.py:204
  836.0 6.5 add_add_fusion.4
  (258 shorter events, 136.8 us)
Async XLA Ops:
  8.0 198.5 %all-reduce.7.cloned.1.call-start = ((), (), s32[]{:S(2)}) async-start(), calls=%async_computation | async-start | bytes 9437184 | tf_op jit(solution)/shard_map/psum | solution.py:138
  91.2 6.7 copy-start.29
  97.9 12.0 %copy-start.8 = (bf16[192,768]{0,1:T(8,128)(2,1)S(1)}, bf16[192,768]{0,1:T(8,128)(2,1)}, u32[]{:S(2)}) copy-start(bf16[192,768]{0,1:T(8,128)(2,1)} %all_gather.19) | copy-start | bytes 884740
  113.0 101.5 %all-gather.5.cloned.1.call-start = ((), (), s32[]{:S(2)}) async-start(), calls=%async_computation.1 | async-start | bytes 1327104 | tf_op jit(solution)/shard_map/all_gather | solution.py:110
  113.8 115.8 %all-gather.7.cloned.1.call-start = ((), (), s32[]{:S(2)}) async-start(), calls=%async_computation.2 | async-start | bytes 1327104 | tf_op jit(solution)/shard_map/all_gather | solution.py:111
  114.5 215.6 %all-reduce.9.cloned.1.call-start = ((), (), s32[]{:S(2)}) async-start(), calls=%async_computation.3 | async-start | bytes 9437184 | tf_op jit(solution)/shard_map/psum | solution.py:147
  235.8 213.6 %all-reduce.11.cloned.1.call-start = ((), (), s32[]{:S(2)}) async-start(), calls=%async_computation.4 | async-start | bytes 9437184 | tf_op jit(solution)/shard_map/psum | solution.py:168
  338.7 6.5 slice-start
  338.7 6.5 slice-start.2
  338.8 6.5 slice-start.1
  338.8 6.5 slice-start.3
  345.3 5.5 copy-start.35
  355.1 406.2 %all-reduce.13.cloned.1.call-start = ((), (), s32[]{:S(2)}) async-start(), calls=%async_computation.6 | async-start | bytes 14155776 | tf_op jit(solution)/shard_map/psum | solution.py:215
  355.2 6.1 copy-start.12
  355.2 6.1 copy-start.37
  525.6 300.0 %all-gather.9.cloned.1.call-start = ((), (), s32[]{:S(2)}) async-start(), calls=%async_computation.5 | async-start | bytes 23592960 | tf_op jit(solution)/shard_map/all_gather | solution.py:204
  532.0 238.6 %copy-start.23 = (f32[3,96,192]{2,1,0:T(8,128)S(1)}, f32[3,96,192]{2,1,0:T(8,128)}, u32[]{:S(2)}) copy-start(f32[3,96,192]{2,1,0:T(8,128)} %param.41) | copy-start | bytes 663556
  532.0 286.0 %copy-start.31 = (f32[6,768]{1,0:T(8,128)S(1)}, f32[6,768]{1,0:T(8,128)}, u32[]{:S(2)}) copy-start(f32[6,768]{1,0:T(8,128)} %param.47) | copy-start | bytes 55300
  532.0 287.4 %copy-start.21 = (f32[192,96]{1,0:T(8,128)S(1)}, f32[192,96]{1,0:T(8,128)}, u32[]{:S(2)}) copy-start(f32[192,96]{1,0:T(8,128)} %param.34) | copy-start | bytes 221188
  532.1 289.3 %copy-start.17 = (f32[768,96]{0,1:T(8,128)S(1)}, f32[768,96]{0,1:T(8,128)}, u32[]{:S(2)}) copy-start(f32[768,96]{0,1:T(8,128)} %param.36) | copy-start | bytes 884740
  532.1 289.3 %copy-start.24 = (f32[768,96]{0,1:T(8,128)S(1)}, f32[768,96]{0,1:T(8,128)}, u32[]{:S(2)}) copy-start(f32[768,96]{0,1:T(8,128)} %param.40) | copy-start | bytes 884740
  532.1 289.2 %copy-start.25 = (f32[768,96]{0,1:T(8,128)S(1)}, f32[768,96]{0,1:T(8,128)}, u32[]{:S(2)}) copy-start(f32[768,96]{0,1:T(8,128)} %param.44) | copy-start | bytes 884740
  534.6 288.8 %copy-start.19 = (f32[96,768]{1,0:T(8,128)S(1)}, f32[96,768]{1,0:T(8,128)}, u32[]{:S(2)}) copy-start(f32[96,768]{1,0:T(8,128)} %param.35) | copy-start | bytes 884740
  534.7 288.8 %copy-start.26 = (f32[96,768]{1,0:T(8,128)S(1)}, f32[96,768]{1,0:T(8,128)}, u32[]{:S(2)}) copy-start(f32[96,768]{1,0:T(8,128)} %param.39) | copy-start | bytes 884740
  (31 other events, 79.0 us)
Sparse Core Ops, SparseCore 0:
  113.1 93.3 all-reduce.6
  235.9 94.1 all-reduce.8
  355.2 94.1 all-reduce.10
  532.1 120.0 all-gather.8
Sparse Core Ops, SparseCore 1:
  116.3 40.8 all-gather.4
  159.8 39.9 all-gather.6
  525.7 235.6 all-reduce.12
